TPU v7x, 32 devices: a whole 2x2x4 slice. The times are simulated.
32 devices in a mesh: batch: 4 (over x, core), cache: 8 (over z, y).
Axes of the slice: x: 2, y: 2, z: 4, core: 2. Of those that a mesh axis runs over, the one named last changes fastest.
Arguments:
- arrivals: bfloat16 [16, 4, 4096], P('batch', None, 'cache'), may hold values from -6 to 6
- norm_gain: float32 [4096], replicated, may hold values from 0.25 to 1.75
- qkv_weight: bfloat16 [4096, 6144], P(None, 'cache'), may hold values from -0.09375 to 0.09375
- out_weight: bfloat16 [4096, 4096], P('cache'), may hold values from -0.09375 to 0.09375
- kv_cache: bfloat16 [16, 16, 2, 8, 128, 128], P('batch', 'cache'), as said below
- slot: int32 [16], replicated, may hold values from 0 to 15, each once
- positions: int32 [16], P('batch'), may hold values from 1664 to 2044
- tile_lists: int32 [16, 8], P('batch'), may hold values from 0 to 15, as said below
Outputs:
- attended: bfloat16 [16, 4, 4096], P('batch', None, 'cache')
Inputs may be any that keep to these rules, and one draw needn't show every extreme that they name: `tile_lists`: tiles of a row are distinct; the first is the tile of position positions - 1, the others lie at most 12 tiles before it. `kv_cache`: entries are of magnitude at most 240.
All inputs are finite; a program needn't handle non-finite values.
Results may differ from a plain program's by a relative error of at most 0.022.
Values may be sent and summed in bfloat16 or wider, within the bound.
A program may use at most 64 MiB of HBM per device.

v0:
```python
import math

import jax
import jax.numpy as jnp
from jax import lax
from jax.sharding import PartitionSpec as P

HEADS = 32
KVH = 8
HD = 128
TILE = 128
IMW = 64
CW = 16


epsilon = 1e-05
very_low = -1e30


def window_mask(query_pos, key_pos):
    return jnp.abs(key_pos % IMW - query_pos % IMW) <= CW


def shards(arrivals, norm_gain, qkv_weight, out_weight, kv_cache, slot, positions, tile_lists):
    row_count = positions.shape[0]
    step_count = arrivals.shape[1]
    groups = HEADS // KVH
    head_share = out_weight.shape[0] // HD
    head_start = lax.axis_index("cache") * head_share
    everyone = lax.all_gather(arrivals, "batch", axis=0, tiled=True)
    inverse = jnp.argsort(slot)
    my_rows = lax.dynamic_slice_in_dim(inverse, lax.axis_index("batch") * row_count, row_count)
    picked = jnp.take(everyone, my_rows, axis=0)
    whole = lax.all_gather(picked, "cache", axis=2, tiled=True)
    wide_values = whole.astype(jnp.float32)
    normed = (
        wide_values
        * lax.rsqrt(jnp.mean(wide_values * wide_values, axis=-1, keepdims=True) + epsilon)
        * norm_gain
    ).astype(jnp.bfloat16)
    projected = jnp.dot(
        normed.reshape(row_count * step_count, -1), qkv_weight, preferred_element_type=jnp.float32
    )
    projected = projected.astype(jnp.bfloat16).reshape(row_count, step_count, -1)
    heads_all = lax.all_gather(projected, "cache", axis=2, tiled=True).reshape(
        row_count, step_count, KVH, groups + 2, HD
    )
    queries = heads_all[:, :, :, :groups, :]
    new_keys = heads_all[:, :, :, groups, :]
    new_vals = heads_all[:, :, :, groups + 1, :]
    score_scale = 1.0 / math.sqrt(HD)
    tiles_here = kv_cache.shape[1]
    tile_ids = lax.axis_index("cache") * tiles_here + jnp.arange(tiles_here, dtype=jnp.int32)
    listed = jnp.any(tile_lists[:, :, None] == tile_ids[None, None, :], axis=1)
    key_pos = tile_ids[:, None] * TILE + jnp.arange(TILE, dtype=jnp.int32)[None, :]
    step_index = jnp.arange(step_count, dtype=jnp.int32)
    query_pos = positions[:, None] + step_index[None, :]
    key_valid = listed[:, None, :, None] & (key_pos[None, None] < positions[:, None, None, None])
    key_valid = key_valid & window_mask(query_pos[:, :, None, None], key_pos[None, None])
    valid_wide = key_valid[:, None, None]
    scores = (
        jnp.einsum(
            "bsjgd,btjkd->bjgstk", queries, kv_cache[:, :, 0], preferred_element_type=jnp.float32
        )
        * score_scale
    )
    new_valid = (step_index[None, :, None] >= step_index[None, None, :]) & window_mask(
        query_pos[:, :, None], query_pos[:, None, :]
    )
    new_scores = (
        jnp.einsum("bsjgd,bujd->bjgsu", queries, new_keys, preferred_element_type=jnp.float32)
        * score_scale
    )
    new_max = jnp.max(jnp.where(new_valid[:, None, None], new_scores, -jnp.inf), axis=-1)
    local_max = jnp.max(jnp.where(valid_wide, scores, very_low), axis=(-2, -1))
    values_here = kv_cache[:, :, 1]

    def own_heads(array):
        merged = array.reshape((row_count, HEADS) + array.shape[3:])
        return lax.dynamic_slice_in_dim(merged, head_start, head_share, 1)

    weights = jnp.where(valid_wide, jnp.exp(scores - local_max[..., None, None]), 0.0)
    totals = jnp.sum(weights, axis=(-2, -1))
    numerator = jnp.einsum(
        "bjgstk,btjkd->bjgsd",
        weights.astype(jnp.bfloat16),
        values_here,
        preferred_element_type=jnp.float32,
    )
    part_sums, part_totals, part_peaks = (
        lax.all_to_all(
            numerator.reshape(1, row_count, HEADS, step_count, HD).astype(jnp.bfloat16),
            "cache",
            split_axis=2,
            concat_axis=0,
            tiled=True,
        ).astype(jnp.float32),
        lax.all_to_all(
            totals.reshape(1, row_count, HEADS, step_count).astype(jnp.bfloat16),
            "cache",
            split_axis=2,
            concat_axis=0,
            tiled=True,
        ).astype(jnp.float32),
        lax.all_to_all(
            local_max.reshape(1, row_count, HEADS, step_count).astype(jnp.bfloat16),
            "cache",
            split_axis=2,
            concat_axis=0,
            tiled=True,
        ).astype(jnp.float32),
    )
    top_own = jnp.maximum(jnp.max(part_peaks, axis=0), own_heads(new_max))
    factor = jnp.exp(part_peaks - top_own[None])
    numer_own = jnp.sum(part_sums * factor[..., None], axis=0)
    total_own = jnp.sum(part_totals * factor, axis=0)
    own_new = own_heads(new_scores)
    new_weights = jnp.where(new_valid[:, None], jnp.exp(own_new - top_own[..., None]), 0.0)
    own_vals = lax.dynamic_slice_in_dim(
        jnp.repeat(new_vals, groups, axis=2), head_start, head_share, 2
    )
    total_all = total_own + jnp.sum(new_weights, axis=-1)
    numer_all = numer_own + jnp.einsum(
        "bhsu,buhd->bhsd",
        new_weights.astype(jnp.bfloat16),
        own_vals,
        preferred_element_type=jnp.float32,
    )
    attention = (numer_all / total_all[..., None]).astype(jnp.bfloat16)
    attn_flat = attention.transpose(0, 2, 1, 3).reshape(row_count * step_count, head_share * HD)
    partial_out = jnp.dot(attn_flat, out_weight, preferred_element_type=jnp.float32).reshape(
        row_count, step_count, -1
    )
    return lax.psum_scatter(
        partial_out.astype(jnp.bfloat16), "cache", scatter_dimension=2, tiled=True
    )


def solution(mesh):
    in_specs = (
        P("batch", None, "cache"),
        P(),
        P(None, "cache"),
        P("cache", None),
        P("batch", "cache", None, None, None, None),
        P(),
        P("batch"),
        P("batch", None),
    )
    out_specs = P("batch", None, "cache")
    return jax.shard_map(shards, mesh=mesh, in_specs=in_specs, out_specs=out_specs, check_vma=False)
```

profile of v0, /device:TPU:0, one launch (start us, length us, event | category | flops | bytes accessed | tf_op | source)
XLA Modules:
  0.0 208.3 jit_solution(18391242171131757612)
XLA Ops:
  6.5 0.9 compare_reduce_fusion
  7.4 0.1 copy.89
  7.5 0.7 add_select_fusion
  8.4 1.9 sort.17
  10.3 6.5 %all_gather.9 = bf16[16,4,512]{2,1,0:T(4,128)(2,1)S(1)} all-gather(bf16[4,4,512]{2,1,0:T(4,128)(2,1)} %param.8), channel_id=1, replica_groups=mesh['batch'=4,'cache'=8] {'batch'}, dimensions={0}, use_global_device_ids=true | all-gather | bytes 81920 | tf_op jit(solution)/shard_map/all_gather | solution.py:30
  16.8 0.6 gather_fusion
  17.4 0.1 broadcast_select_fusion
  17.5 31.3 %all_gather.10 = bf16[4,4,4096]{2,1,0:T(4,128)(2,1)S(1)} all-gather(bf16[4,4,512]{2,1,0:T(4,128)(2,1)S(1)} %broadcast_select_fusion), channel_id=1, replica_groups=mesh['batch'=4,'cache'=8] {'cache'}, dimensions={2}, use_global_device_ids=true | all-gather | bytes 147456 | tf_op jit(solution)/shard_map/all_gather | solution.py:34
  48.8 0.2 fusion.14
  49.0 0.9 fusion.16
  49.9 3.7 %convolution_convert_fusion.1 = bf16[16,768]{1,0:T(8,128)(2,1)S(1)} fusion(bf16[16,4096]{1,0:T(8,128)(2,1)S(1)} %reshape.312, bf16[4096,768]{1,0:T(8,128)(2,1)} %param.10), kind=kOutput, calls=%fused_computation.13 | convolution fusion | flops 100675584 | bytes 6447104 | tf_op jit(solution)/shard_map/dot_general | solution.py:41
  53.6 30.7 %all_gather.11 = bf16[4,4,6144]{2,1,0:T(4,128)(2,1)S(1)} all-gather(bf16[4,4,768]{2,1,0:T(4,128)(2,1)S(1)} %reshape.313), channel_id=1, replica_groups=mesh['batch'=4,'cache'=8] {'cache'}, dimensions={2}, use_global_device_ids=true | all-gather | bytes 221184 | tf_op jit(solution)/shard_map/all_gather | solution.py:45
  84.3 0.2 reshape.314
  84.5 2.6 %fusion.37 = (bf16[4,2,1,8,128,128]{5,4,3,2,1,0:T(8,128)(2,1)S(1)}, bf16[4,2,1,8,128,128]{5,4,3,2,1,0:T(8,128)(2,1)S(1)}) fusion(bf16[4,2,2,8,128,128]{5,4,3,2,1,0:T(8,128)(2,1)} %param.12), kind=kLoop, calls=%fused_computation.74 | loop fusion | bytes 8388608 | tf_op jit(solution)/shard_map/slice | solution.py:76
  87.3 0.1 compare_and_fusion
  87.4 0.8 select_reduce_fusion
  88.1 0.2 copy.95
  88.3 0.8 copy.116
  89.1 5.5 %all-to-all-start.1 = ((bf16[1,4,32,4]{3,1,0,2:T(4,128)(2,1)}), bf16[1,4,32,4]{3,1,0,2:T(4,128)(2,1)S(1)}, u32[]{:S(2)}, u32[]{:S(2)}) async-start(bf16[1,4,32,4]{3,1,0,2:T(4,128)(2,1)} %bitcast.15), calls=%async_computation.1 | async-start | bytes 65536 | tf_op jit(solution)/shard_map/all_to_all | solution.py:105
  94.6 0.1 fusion.38
  94.8 0.5 fusion.12
  95.3 0.4 fusion.7
  95.7 1.3 select_reduce_fusion.1
  97.1 0.1 reshape.315
  97.2 0.1 copy.102
  97.3 0.1 reshape.316
  97.4 0.2 copy.106
  97.6 0.7 copy.94
  98.3 0.8 copy.120
  99.1 2.2 %all-to-all-done.1 = bf16[1,4,32,4]{3,1,0,2:T(4,128)(2,1)S(1)} async-done(((bf16[1,4,32,4]{3,1,0,2:T(4,128)(2,1)}), bf16[1,4,32,4]{3,1,0,2:T(4,128)(2,1)S(1)}, u32[]{:S(2)}, u32[]{:S(2)}) %all-to-all-start.1) | async-done | bytes 1056 | tf_op jit(solution)/shard_map/all_to_all | solution.py:105
  101.3 3.8 %all-to-all-start.2 = ((bf16[1,4,32,4]{3,1,0,2:T(4,128)(2,1)}), bf16[1,4,32,4]{3,1,0,2:T(4,128)(2,1)S(1)}, u32[]{:S(2)}, u32[]{:S(2)}) async-start(bf16[1,4,32,4]{3,1,0,2:T(4,128)(2,1)} %bitcast.26), calls=%async_computation.2 | async-start | bytes 65536 | tf_op jit(solution)/shard_map/all_to_all | solution.py:98
  105.1 0.3 copy.117
  105.4 6.3 %all-to-all-done.2 = bf16[1,4,32,4]{3,1,0,2:T(4,128)(2,1)S(1)} async-done(((bf16[1,4,32,4]{3,1,0,2:T(4,128)(2,1)}), bf16[1,4,32,4]{3,1,0,2:T(4,128)(2,1)S(1)}, u32[]{:S(2)}, u32[]{:S(2)}) %all-to-all-start.2) | async-done | bytes 1056 | tf_op jit(solution)/shard_map/all_to_all | solution.py:98
  111.8 3.4 %all-to-all-start = ((bf16[1,4,32,4,128]{4,3,1,0,2:T(4,128)(2,1)}), bf16[1,4,32,4,128]{4,3,1,0,2:T(4,128)(2,1)S(1)}, u32[]{:S(2)}, u32[]{:S(2)}) async-start(bf16[1,4,32,4,128]{4,3,1,0,2:T(4,128)(2,1)} %copy.94), calls=%async_computation | async-start | bytes 262144 | tf_op jit(solution)/shard_map/all_to_all | solution.py:91
  115.2 0.1 copy.109
  115.4 0.1 dynamic-slice_maximum_fusion
  115.5 0.1 fusion.27
  115.6 0.2 copy.104
  115.9 0.1 copy.110
  116.0 0.3 copy.101
  116.3 6.1 %all-to-all-done = bf16[1,4,32,4,128]{4,3,1,0,2:T(4,128)(2,1)S(1)} async-done(((bf16[1,4,32,4,128]{4,3,1,0,2:T(4,128)(2,1)}), bf16[1,4,32,4,128]{4,3,1,0,2:T(4,128)(2,1)S(1)}, u32[]{:S(2)}, u32[]{:S(2)}) %all-to-all-start) | async-done | bytes 131104 | tf_op jit(solution)/shard_map/all_to_all | solution.py:91
  122.4 0.2 fusion.17
  122.7 3.0 %convolution_convert_fusion = bf16[4,4,4096]{2,1,0:T(4,128)(2,1)S(1)} fusion(bf16[512,4096]{1,0:T(8,128)(2,1)} %param.11, bf16[4,4,4,4]{3,2,1,0:T(4,128)(2,1)S(1)} %copy.104, f32[4,4,4,128]{3,2,0,1:T(4,128)S(1)} %fusion.17, f32[4,4,4]{1,2,0:T(4,128)S(1)} %copy.110, bf16[4,4,32,128]{3,1,2,0:T(4,128)(2,1)S(1)} %bitcast.113, s32[]{:T(128)S(6)} %select_n.81), kind=kOutput, calls=%fused_computation.1 | convolution fusion | flops 67264512 | bytes 4399108 | tf_op jit(solution)/shard_map/dot_general | solution.py:131
  125.7 4.8 %copy.121 = bf16[4,4,4096]{1,0,2:T(4,128)(2,1)} copy(bf16[4,4,4096]{2,1,0:T(4,128)(2,1)S(1)} %convolution_convert_fusion) | data formatting | bytes 262144
  130.5 6.1 %reshape.338 = bf16[4096,16]{1,0:T(8,128)(2,1)} reshape(bf16[4096,4,4]{2,1,0:T(4,128)(2,1)} %bitcast.110) | data formatting | bytes 262144
  136.6 62.8 %reduce-scatter.4.cloned.1.call-done = bf16[512,16]{1,0:T(8,128)(2,1)} async-done(((bf16[4096,16]{1,0:T(8,128)(2,1)}), bf16[512,16]{1,0:T(8,128)(2,1)}) %reduce-scatter.4.cloned.1.call-update) | async-done | bytes 16400
  199.3 1.1 reshape.339
  200.5 0.9 copy.122
  (22 shorter events, 0.7 us)
Async XLA Ops:
  84.5 2.6 %copy-start = (s32[4]{0:T(128)S(1)}, s32[4]{0:T(128)}, u32[]{:S(2)}) copy-start(s32[4]{0:T(128)} %param.14) | copy-start | bytes 52
  89.1 12.2 %all-to-all-start.1 = ((bf16[1,4,32,4]{3,1,0,2:T(4,128)(2,1)}), bf16[1,4,32,4]{3,1,0,2:T(4,128)(2,1)S(1)}, u32[]{:S(2)}, u32[]{:S(2)}) async-start(bf16[1,4,32,4]{3,1,0,2:T(4,128)(2,1)} %bitcast.15), calls=%async_computation.1 | async-start | bytes 65536 | tf_op jit(solution)/shard_map/all_to_all | solution.py:105
  101.3 10.5 %all-to-all-start.2 = ((bf16[1,4,32,4]{3,1,0,2:T(4,128)(2,1)}), bf16[1,4,32,4]{3,1,0,2:T(4,128)(2,1)S(1)}, u32[]{:S(2)}, u32[]{:S(2)}) async-start(bf16[1,4,32,4]{3,1,0,2:T(4,128)(2,1)} %bitcast.26), calls=%async_computation.2 | async-start | bytes 65536 | tf_op jit(solution)/shard_map/all_to_all | solution.py:98
  111.8 10.7 %all-to-all-start = ((bf16[1,4,32,4,128]{4,3,1,0,2:T(4,128)(2,1)}), bf16[1,4,32,4,128]{4,3,1,0,2:T(4,128)(2,1)S(1)}, u32[]{:S(2)}, u32[]{:S(2)}) async-start(bf16[1,4,32,4,128]{4,3,1,0,2:T(4,128)(2,1)} %copy.94), calls=%async_computation | async-start | bytes 262144 | tf_op jit(solution)/shard_map/all_to_all | solution.py:91
  115.1 84.2 %reduce-scatter.4.cloned.1.call-start = ((), (), s32[]{:S(2)}) async-start(), calls=%async_computation.4 | async-start | bytes 1179648
Sparse Core Ops, SparseCore 0:
  136.7 62.6 reduce-scatter.3
where the time goes:
time: 209 us; the launch traced here: 208 us
  waiting for transfers between devices  77.5 us (37%)
  blocking collectives  68.5 us (33%)
  local copies, waits for them, and re-layouts  20.8 us (10%)
  between operations  13.6 us (7%)
  starting transfers between devices  12.7 us (6%)
  matrix products  9.2 us (4%)
  other arithmetic  6.06 us (3%)
    unnamed x2, waiting for transfers between devices  62.8 us
    all_gather x1, blocking collectives, shards(): whole = lax.all_gather(picked, 'cache', axis=2, tiled=True)  31.3 us
    all_gather x1, blocking collectives, shards(): lax.all_gather(projected, 'cache', axis=2, tiled=True)  30.7 us
    unnamed x6, local copies, waits for them, and re-layouts  12.9 us
    all_gather x1, blocking collectives, shards(): everyone = lax.all_gather(arrivals, 'batch', axis=0, tiled=True)  6.46 us
    all_to_all x1, waiting for transfers between devices, shards(): lax.all_to_all(totals.reshape(1, row_count, HEADS, step_count).astype(jnp...  6.33 us
    all_to_all x1, waiting for transfers between devices, shards(): lax.all_to_all(numerator.reshape(1, row_count, HEADS, step_count, HD).ast...  6.14 us
    all_to_all x1, starting transfers between devices, shards(): lax.all_to_all(local_max.reshape(1, row_count, HEADS, step_count).astype(...  5.49 us
  transfers between devices with their start and end apart: 4, of which 4 were waited for; matrix products, arithmetic and copies ran while one was open for 3% of the time, Pallas kernels for 0%

commit v1 on v0

v1 whole, which is shorter than its diff:
```python
import functools
import math

import jax
import jax.numpy as jnp
from jax import lax
from jax.experimental import pallas as pl
from jax.experimental.pallas import tpu as pltpu
from jax.sharding import PartitionSpec as P

HEADS = 32
KVH = 8
HD = 128
TILE = 128
IMW = 64
CW = 16
GROUPS = HEADS // KVH

epsilon = 1e-05
very_low = -1e30
f32 = jnp.float32
bf16 = jnp.bfloat16


def kernel(nb, n, slot, pos, lists, arr, gain, wq_hbm, wo_hbm, kv_hbm, out,
           wq, wo, kv, abuf, xrow, xg, prow, pg, pn, ps, arow, po, ro,
           wsem, ssem, rsem, bssem, brsem):
    b = lax.axis_index("batch")
    me = lax.axis_index("cache")
    rows, steps, feat = arr.shape
    depth, cols = wq_hbm.shape
    hs = wo_hbm.shape[0] // HD
    tiles = kv_hbm.shape[1]
    grp = cols // HD
    per = (GROUPS + 2) // grp
    hq = hs * steps
    toks = rows * steps
    nq = rows * hq

    loads_q = [
        pltpu.make_async_copy(wq_hbm.at[pl.ds(c * feat, feat)], wq.at[c], wsem.at[c])
        for c in range(n)
    ]
    load_kv = [
        pltpu.make_async_copy(kv_hbm.at[r], kv.at[r], wsem.at[n + r]) for r in range(rows)
    ]
    loads_o = [
        pltpu.make_async_copy(wo_hbm.at[:, pl.ds(c * feat, feat)], wo.at[c], wsem.at[n + rows + c])
        for c in range(n)
    ]
    own = pltpu.make_async_copy(arr, abuf.at[pl.ds(b * rows, rows)], wsem.at[2 * n + rows])
    own.start()
    for c in loads_q:
        c.start()

    barrier = pltpu.get_barrier_semaphore()
    for k in range(1, nb):
        pl.semaphore_signal(barrier, inc=1, device_id=(lax.rem(b + k, nb), me),
                            device_id_type=pl.DeviceIdType.MESH)
    for k in range(1, n):
        pl.semaphore_signal(barrier, inc=1, device_id=(b, lax.rem(me + k, n)),
                            device_id_type=pl.DeviceIdType.MESH)
    pl.semaphore_wait(barrier, nb + n - 2)

    def exchange(src, dst, phase, k, to):
        return pltpu.make_async_remote_copy(
            src_ref=src, dst_ref=dst, send_sem=ssem.at[phase, k], recv_sem=rsem.at[phase, k],
            device_id=(b, to), device_id_type=pl.DeviceIdType.MESH)

    def batch_copy(k, at):
        return pltpu.make_async_remote_copy(
            src_ref=arr, dst_ref=abuf.at[pl.ds(at * rows, rows)], send_sem=bssem.at[k],
            recv_sem=brsem.at[k], device_id=(lax.rem(b + k, nb), me),
            device_id_type=pl.DeviceIdType.MESH)

    for k in range(1, nb):
        batch_copy(k, b).start()
    for c in load_kv + loads_o:
        c.start()
    own.wait()
    for k in range(1, nb):
        batch_copy(k, lax.rem(b + nb - k, nb)).wait_recv()
    for r in range(rows):
        place = jnp.int32(0)
        for i in range(nb * rows):
            place = jnp.where(slot[i] == b * rows + r, i, place)
        xrow[r * steps:(r + 1) * steps, :] = abuf[place].astype(f32)
    xg[me] = xrow[...].astype(bf16)
    for k in range(1, n):
        exchange(xg.at[me], xg.at[me], 0, k, lax.rem(me + k, n)).start()
    for k in range(1, n):
        frm = lax.rem(me + n - k, n)
        exchange(xg.at[frm], xg.at[frm], 0, k, lax.rem(me + k, n)).wait_recv()

    square = jnp.zeros((toks, 1), f32)
    for c in range(n):
        x = xg[c].astype(f32)
        square = square + jnp.sum(x * x, axis=1, keepdims=True)
    scale = lax.rsqrt(square / depth + epsilon)
    acc = jnp.zeros((toks, cols), f32)
    for c in range(n):
        loads_q[c].wait()
        y = (xg[c].astype(f32) * scale * gain[:, c * feat:(c + 1) * feat]).astype(bf16)
        acc = acc + jnp.dot(y, wq[c], preferred_element_type=f32)
    for r in range(rows):
        for g in range(grp):
            prow[r, g * steps:(g + 1) * steps, :] = acc[r * steps:(r + 1) * steps,
                                                        g * HD:(g + 1) * HD]
    pg[me] = prow[...].astype(bf16)
    for k in range(1, n):
        exchange(pg.at[me], pg.at[me], 1, k, lax.rem(me + k, n)).start()

    q_rows = GROUPS * steps
    row_i = lax.broadcasted_iota(jnp.int32, (q_rows, TILE), 0)
    lane_i = lax.broadcasted_iota(jnp.int32, (q_rows, TILE), 1)
    masks = []
    for r in range(rows):
        p = pos[r]
        near = jnp.abs((lane_i & (IMW - 1)) - ((p + (row_i & (steps - 1))) & (IMW - 1))) <= CW
        per_tile = []
        for t in range(tiles):
            tile_id = me * tiles + t
            hit = jnp.int32(0)
            for w in range(lists.shape[1]):
                hit = hit + jnp.where(lists[r, w] == tile_id, 1, 0)
            limit = jnp.where(hit > 0, p - tile_id * TILE, 0)
            per_tile.append(near & (lane_i < limit))
        masks.append(per_tile)

    for k in range(1, n):
        frm = lax.rem(me + n - k, n)
        exchange(pg.at[frm], pg.at[frm], 1, k, lax.rem(me + k, n)).wait_recv()
    for c in load_kv:
        c.wait()

    score_scale = 1.0 / math.sqrt(HD)
    dests = GROUPS // hs
    my_j = me // dests

    def head_rows(j, r):
        if per == 1:
            return pg[j, r, 0:q_rows, :]
        first = pg[per * j, r].astype(f32)
        second = pg[per * j + 1, r].astype(f32)
        return jnp.concatenate([first, second[0:q_rows - grp * steps]], axis=0).astype(bf16)

    def one_head(i, carry):
        j = lax.rem(my_j + 1 + i, KVH)
        peaks = jnp.zeros((q_rows, TILE), f32)
        totals = jnp.zeros((q_rows, TILE), f32)
        for r in range(rows):
            q = head_rows(j, r)
            s = []
            for t in range(tiles):
                raw = lax.dot_general(q, kv[r, t, 0, j], (((1,), (1,)), ((), ())),
                                      preferred_element_type=f32) * score_scale
                s.append(jnp.where(masks[r][t], raw, very_low))
            best = s[0]
            for t in range(1, tiles):
                best = jnp.maximum(best, s[t])
            peak = jnp.max(best, axis=1, keepdims=True)
            num = jnp.zeros((q_rows, HD), f32)
            mass = jnp.zeros((q_rows, TILE), f32)
            for t in range(tiles):
                w = jnp.where(masks[r][t], jnp.exp(s[t] - peak), 0.0)
                mass = mass + w
                num = num + jnp.dot(w.astype(bf16), kv[r, t, 1, j], preferred_element_type=f32)
            total = jnp.sum(mass, axis=1, keepdims=True)
            here = lane_i == r * hq + lax.rem(row_i, hq)
            peaks = peaks + jnp.where(here, peak, 0.0)
            totals = totals + jnp.where(here, total, 0.0)
            for e in range(dests):
                pn[dests * j + e, r] = num[e * hq:(e + 1) * hq].astype(bf16)
        for e in range(dests):
            d = dests * j + e
            pk = jnp.sum(peaks[e * hq:(e + 1) * hq], axis=0, keepdims=True)
            tt = jnp.sum(totals[e * hq:(e + 1) * hq], axis=0, keepdims=True)
            sub = lax.broadcasted_iota(jnp.int32, (8, TILE), 0)
            ps[d] = jnp.where(sub == 0, pk, tt)

            @pl.when(d != me)
            def _():
                k = lax.rem(d - me + n, n)
                exchange(pn.at[d], ro_n.at[me], 2, k, d).start()
                exchange(ps.at[d], ro_s.at[me], 3, k, d).start()
        return carry

    ro_n, ro_s = ro
    lax.fori_loop(0, KVH, one_head, 0)
    ro_n[me] = pn[me]
    ro_s[me] = ps[me]

    if per == 1:
        q_own = pg[my_j, :, 0:q_rows, :].reshape(nq, HD)
        kv_own = pg[my_j, :, q_rows:q_rows + 2 * steps, :].astype(f32)
    else:
        first = pg[per * my_j].astype(f32)
        second = pg[per * my_j + 1].astype(f32)
        q_all = jnp.concatenate([first, second[:, 0:q_rows - grp * steps]], axis=1)
        part = lax.rem(me, dests)
        q_own = q_all[:, 0:hq]
        for e in range(1, dests):
            q_own = jnp.where(part == e, q_all[:, e * hq:(e + 1) * hq], q_own)
        q_own = q_own.reshape(nq, HD).astype(bf16)
        off = q_rows - grp * steps
        kv_own = second[:, off:off + 2 * steps]
    kv_own = kv_own.reshape(rows * 2 * steps, HD)
    new_k = kv_own.astype(bf16)
    new_v = pltpu.roll(kv_own, rows * 2 * steps - steps, 0).astype(bf16)
    nk = rows * 2 * steps
    qi = lax.broadcasted_iota(jnp.int32, (nq, nk), 0)
    ki = lax.broadcasted_iota(jnp.int32, (nq, nk), 1)
    q_req, k_req = qi // hq, ki // (2 * steps)
    qs, ku = qi & (steps - 1), ki & (2 * steps - 1)
    p_vec = jnp.zeros((nq, nk), jnp.int32)
    for r in range(rows):
        p_vec = jnp.where(q_req == r, pos[r], p_vec)
    valid = (q_req == k_req) & (ku <= qs) & (
        jnp.abs(((p_vec + ku) & (IMW - 1)) - ((p_vec + qs) & (IMW - 1))) <= CW)
    s_new = lax.dot_general(q_own, new_k, (((1,), (1,)), ((), ())),
                            preferred_element_type=f32) * score_scale
    top_new = jnp.max(jnp.where(valid, s_new, very_low), axis=1, keepdims=True)
    diag = (lax.broadcasted_iota(jnp.int32, (nq, TILE), 0)
            == lax.broadcasted_iota(jnp.int32, (nq, TILE), 1))
    top = jnp.sum(jnp.where(diag, top_new, 0.0), axis=0, keepdims=True)

    def column(line):
        return jnp.sum(jnp.where(diag, line, 0.0), axis=1, keepdims=True)

    for k in range(1, n):
        frm = lax.rem(me + n - k, n)
        exchange(ps.at[frm], ro_s.at[frm], 3, k, lax.rem(me + k, n)).wait_recv()
    for c in range(n):
        top = jnp.maximum(top, ro_s[c, 0:1, :])
    total = jnp.zeros((1, TILE), f32)
    factors = []
    for c in range(n):
        f = jnp.exp(ro_s[c, 0:1, :] - top)
        total = total + ro_s[c, 1:2, :] * f
        factors.append(column(f))
    w_new = jnp.where(valid, jnp.exp(s_new - column(top)), 0.0)
    total = column(total) + jnp.sum(w_new, axis=1, keepdims=True)
    numer = jnp.dot(w_new.astype(bf16), new_v, preferred_element_type=f32)
    for k in range(1, n):
        frm = lax.rem(me + n - k, n)
        exchange(pn.at[frm], ro_n.at[frm], 2, k, lax.rem(me + k, n)).wait_recv()
    for c in range(n):
        numer = numer + ro_n[c].astype(f32).reshape(nq, HD) * factors[c]
    attn = numer / total
    for r in range(rows):
        for g in range(hs):
            at = r * hq + g * steps
            arow[r * steps:(r + 1) * steps, g * HD:(g + 1) * HD] = attn[at:at + steps]
    flat = arow[...].astype(bf16)
    for c in loads_o:
        c.wait()
    po_s, po_r = po
    for k in range(1, n + 1):
        d = lax.rem(me + k, n)
        part_out = jnp.dot(flat, wo[d], preferred_element_type=f32).astype(bf16)
        if k < n:
            po_s[k] = part_out
            exchange(po_s.at[k], po_r.at[k], 4, k, d).start()
        else:
            result = part_out.astype(f32)
    for k in range(1, n):
        exchange(po_s.at[k], po_r.at[k], 4, k, lax.rem(me + k, n)).wait_recv()
        result = result + po_r[k].astype(f32)
    for r in range(rows):
        out[r] = result[r * steps:(r + 1) * steps].astype(bf16)

    for k in range(1, nb):
        batch_copy(k, b).wait_send()
    for k in range(1, n):
        d = lax.rem(me + k, n)
        exchange(xg.at[me], xg.at[me], 0, k, d).wait_send()
        exchange(pg.at[me], pg.at[me], 1, k, d).wait_send()
        exchange(pn.at[d], ro_n.at[me], 2, k, d).wait_send()
        exchange(ps.at[d], ro_s.at[me], 3, k, d).wait_send()
        exchange(po_s.at[k], po_r.at[k], 4, k, d).wait_send()


def shards(nb, n, arrivals, norm_gain, qkv_weight, out_weight, kv_cache, slot, positions,
           tile_lists):
    rows, steps, feat = arrivals.shape
    depth, cols = qkv_weight.shape
    hs = out_weight.shape[0] // HD
    hq = hs * steps
    grp = cols // HD
    smem = pl.BlockSpec(memory_space=pltpu.SMEM)
    vmem = pl.BlockSpec(memory_space=pltpu.VMEM)
    hbm = pl.BlockSpec(memory_space=pl.ANY)
    dma = pltpu.SemaphoreType.DMA
    return pl.pallas_call(
        functools.partial(kernel, nb, n),
        out_shape=jax.ShapeDtypeStruct(arrivals.shape, bf16),
        in_specs=[smem, smem, smem, vmem, vmem, hbm, hbm, hbm],
        out_specs=vmem,
        scratch_shapes=[
            pltpu.VMEM((n, feat, cols), bf16),
            pltpu.VMEM((n, out_weight.shape[0], feat), bf16),
            pltpu.VMEM(kv_cache.shape, bf16),
            pltpu.VMEM((nb * rows, steps, feat), bf16),
            pltpu.VMEM((rows * steps, feat), f32),
            pltpu.VMEM((n, rows * steps, feat), bf16),
            pltpu.VMEM((rows, grp * steps, HD), f32),
            pltpu.VMEM((n, rows, grp * steps, HD), bf16),
            pltpu.VMEM((n, rows, hq, HD), bf16),
            pltpu.VMEM((n, 8, TILE), f32),
            pltpu.VMEM((rows * steps, hs * HD), f32),
            (pltpu.VMEM((n, rows * steps, feat), bf16), pltpu.VMEM((n, rows * steps, feat), bf16)),
            (pltpu.VMEM((n, rows, hq, HD), bf16), pltpu.VMEM((n, 8, TILE), f32)),
            dma((2 * n + rows + 1,)),
            dma((5, n)),
            dma((5, n)),
            dma((nb,)),
            dma((nb,)),
        ],
        compiler_params=pltpu.CompilerParams(collective_id=0, has_side_effects=True,
                                             vmem_limit_bytes=48 << 20),
    )(slot, positions, tile_lists, arrivals, norm_gain.reshape(1, -1), qkv_weight, out_weight,
      kv_cache)


def solution(mesh):
    in_specs = (
        P("batch", None, "cache"),
        P(),
        P(None, "cache"),
        P("cache", None),
        P("batch", "cache", None, None, None, None),
        P(),
        P("batch"),
        P("batch", None),
    )
    out_specs = P("batch", None, "cache")
    body = functools.partial(shards, mesh.shape["batch"], mesh.shape["cache"])
    return jax.shard_map(body, mesh=mesh, in_specs=in_specs, out_specs=out_specs, check_vma=False)
```

time: 209 us -> 46.4 us (0.22)
  waiting for transfers between devices: 77.5 us -> 0 us
  blocking collectives: 68.5 us -> 0 us
  Pallas kernels: 0 us -> 39.8 us
  local copies, waits for them, and re-layouts: 20.8 us -> 6.22 us
  between operations: 13.6 us -> 0.02 us
  starting transfers between devices: 12.7 us -> 0 us
  matrix products: 9.2 us -> 0 us
  other arithmetic: 6.06 us -> 0 us
    all_gather x3 -> x0, blocking collectives: 68.5 us -> none  [the longest x1 31.3 us: shards(): whole = lax.all_gather(picked, 'cache', axis=2, tiled=True)]
    unnamed x2 -> x0, waiting for transfers between devices: 62.8 us -> none
    pallas_call x0 -> x1, Pallas kernels: none -> 39.8 us  [shards(): pl.pallas_call(functools.partial(kernel, nb, n), out_shape=jax.ShapeDtype...]
    all_to_all x3 -> x0, waiting for transfers between devices: 14.7 us -> none  [the longest x1 6.33 us: shards(): lax.all_to_all(totals.reshape(1, row_count, HEADS, step_count).astype(jnp...]
    all_to_all x3 -> x0, starting transfers between devices: 12.6 us -> none  [the longest x1 5.49 us: shards(): lax.all_to_all(local_max.reshape(1, row_count, HEADS, step_count).astype(...]
    dot_general x5 -> x0, matrix products: 9.2 us -> none  [the longest x1 3.71 us: shards(): jnp.dot(normed.reshape(row_count * step_count, -1), qkv_weight, preferred...]
    unnamed x6 -> x13, local copies, waits for them, and re-layouts: 12.9 us -> 6.22 us
    slice x2 -> x0, local copies, waits for them, and re-layouts: 2.76 us -> none  [the longest x1 2.63 us: shards(): values_here = kv_cache[:, :, 1]]
  transfers between devices with their start and end apart: 4 -> 0, of which waited for: 4 -> 0; matrix products, arithmetic and copies ran while one was open for 3% -> 0% of each run, Pallas kernels for 0% -> 0%
where the time goes in v1:
time: 46.4 us; the launch traced here: 46.1 us
  Pallas kernels  39.8 us (86%)
  local copies, waits for them, and re-layouts  6.22 us (13%)
    pallas_call x1, Pallas kernels, shards(): pl.pallas_call(functools.partial(kernel, nb, n), out_shape=jax.ShapeDtype...  39.8 us
    unnamed x13, local copies, waits for them, and re-layouts  6.22 us

profile of v1, /device:TPU:0, one launch (start us, length us, event | category | flops | bytes accessed | tf_op | source)
XLA Modules:
  0.0 46.1 jit_solution(15427561551611458669)
XLA Ops:
  0.0 0.0 copy-start
  0.0 2.2 %copy-done = bf16[512,4096]{1,0:T(8,128)(2,1)S(1)} copy-done((bf16[512,4096]{1,0:T(8,128)(2,1)S(1)}, bf16[512,4096]{1,0:T(8,128)(2,1)}, u32[]{:S(2)}) %copy-start) | copy-done | bytes 4194328
  2.2 0.0 copy-start.1
  2.2 0.7 %copy-done.1 = bf16[4,4,512]{2,1,0:T(4,128)(2,1)S(1)} copy-done((bf16[4,4,512]{2,1,0:T(4,128)(2,1)S(1)}, bf16[4,4,512]{2,1,0:T(4,128)(2,1)}, u32[]{:S(2)}) %copy-start.1) | copy-done | bytes 16408
  2.9 0.0 copy-start.2
  2.9 0.7 %copy-done.2 = f32[4096]{0:T(1024)S(1)} copy-done((f32[4096]{0:T(1024)S(1)}, f32[4096]{0:T(1024)}, u32[]{:S(2)}) %copy-start.2) | copy-done | bytes 16408
  3.6 0.0 copy-start.3
  3.6 0.7 %copy-done.3 = s32[4,8]{1,0:T(4,128)S(1)} copy-done((s32[4,8]{1,0:T(4,128)S(1)}, s32[4,8]{1,0:T(4,128)}, u32[]{:S(2)}) %copy-start.3) | copy-done | bytes 152
  4.3 0.0 copy-start.4
  4.3 0.7 %copy-done.4 = s32[16]{0:T(128)S(1)} copy-done((s32[16]{0:T(128)S(1)}, s32[16]{0:T(128)}, u32[]{:S(2)}) %copy-start.4) | copy-done | bytes 88
  5.0 0.0 copy-start.5
  5.0 0.7 %copy-done.5 = s32[4]{0:T(128)S(1)} copy-done((s32[4]{0:T(128)S(1)}, s32[4]{0:T(128)}, u32[]{:S(2)}) %copy-start.5) | copy-done | bytes 40
  5.6 39.8 %shard_map.82 = bf16[4,4,512]{2,1,0:T(4,128)(2,1)S(1)} custom-call(s32[16]{0:T(128)S(1)} %copy-done.4, s32[4]{0:T(128)S(1)} %copy-done.5, s32[4,8]{1,0:T(4,128)S(1)} %copy-done.3, bf16[4,4,512]{2,1,0:T(4,128)(2,1)S(1)} %copy-done.1, f32[1,4096]{1,0:T(1,128)S(1)} %bitcast.1, bf16[4096,768]{1,0:T(8,128)(2,1)} %wq_hbm.1, bf16[512,4096]{1,0:T(8,128)(2,1)S(1)} %copy-done, ...), custom_call_target="tpu_custom_call" | custom-call | tf_op jit(solution)/shard_map/pallas_call | solution.py:294
  45.5 0.6 %copy.10 = bf16[4,4,512]{2,1,0:T(4,128)(2,1)} copy(bf16[4,4,512]{2,1,0:T(4,128)(2,1)S(1)} %shard_map.82) | data formatting | bytes 32768
Async XLA Ops:
  0.0 2.2 %copy-start = (bf16[512,4096]{1,0:T(8,128)(2,1)S(1)}, bf16[512,4096]{1,0:T(8,128)(2,1)}, u32[]{:S(2)}) copy-start(bf16[512,4096]{1,0:T(8,128)(2,1)} %wo_hbm.1) | copy-start | bytes 12582916
  2.2 0.7 %copy-start.1 = (bf16[4,4,512]{2,1,0:T(4,128)(2,1)S(1)}, bf16[4,4,512]{2,1,0:T(4,128)(2,1)}, u32[]{:S(2)}) copy-start(bf16[4,4,512]{2,1,0:T(4,128)(2,1)} %arr.1) | copy-start | bytes 49156
  2.9 0.7 %copy-start.2 = (f32[4096]{0:T(1024)S(1)}, f32[4096]{0:T(1024)}, u32[]{:S(2)}) copy-start(f32[4096]{0:T(1024)} %param.9) | copy-start | bytes 49156
  3.6 0.7 %copy-start.3 = (s32[4,8]{1,0:T(4,128)S(1)}, s32[4,8]{1,0:T(4,128)}, u32[]{:S(2)}) copy-start(s32[4,8]{1,0:T(4,128)} %lists.1) | copy-start | bytes 388
  4.3 0.7 %copy-start.4 = (s32[16]{0:T(128)S(1)}, s32[16]{0:T(128)}, u32[]{:S(2)}) copy-start(s32[16]{0:T(128)} %slot.1) | copy-start | bytes 196
  5.0 0.7 %copy-start.5 = (s32[4]{0:T(128)S(1)}, s32[4]{0:T(128)}, u32[]{:S(2)}) copy-start(s32[4]{0:T(128)} %pos.1) | copy-start | bytes 52
